TPU v7x, 32 devices: a whole 2x2x4 slice. The times are simulated.
32 devices in a mesh: dp: 8 (over z, x), tensor: 4 (over y, core).
Axes of the slice: x: 2, y: 2, z: 4, core: 2. Of those that a mesh axis runs over, the one named last changes fastest.
Arguments:
- hidden_in: bfloat16 [8192, 768], P('dp'), may hold values from -6 to 6
- w_qkv: bfloat16 [3, 768, 768], P(None, None, 'tensor'), may hold values from -0.21875 to 0.21875
- w_out: bfloat16 [768, 768], P('tensor'), may hold values from -0.625 to 0.625
- w_ff1: bfloat16 [768, 768], P(None, 'tensor'), may hold values from -0.21875 to 0.21875
- w_ff2: bfloat16 [768, 768], P('tensor'), may hold values from -0.21875 to 0.21875
- ln1_gain: float32 [768], replicated, may hold values from 0.5 to 1.5
- ln1_bias: float32 [768], replicated, may hold values from -3 to 3
- ln2_gain: float32 [768], replicated, may hold values from 0.5 to 1.5
- ln2_bias: float32 [768], replicated, may hold values from -3 to 3
- spd_table: float32 [32, 32], P(None, 'tensor'), may hold values from -3 to 3
- edge_table: float32 [32, 32], P(None, 'tensor'), may hold values from -3 to 3
- kernel_w1: bfloat16 [128, 128], replicated, may hold values from -0.5 to 0.5
- kernel_w2: bfloat16 [128, 32], P(None, 'tensor'), may hold values from -0.5 to 0.5
- centers: float32 [128], replicated, may hold values from 0 to 8
- widths: float32 [128], replicated, may hold values from 0.3 to 3
- atom_count: int32 [128], P('dp'), may hold values from 16 to 64, as said below
- mol_mode: int32 [128], P('dp'), may hold values from 0 to 2
- spd_bucket: int32 [128, 64, 64], P('dp'), may hold values from 0 to 31
- edge_type: int32 [128, 64, 64], P('dp'), may hold values from 0 to 31
- dist_bucket: int32 [128, 64, 64], P('dp'), may hold values from 0 to 127
- cotangent: bfloat16 [8192, 768], P('dp'), may hold values from -6 to 6
Outputs:
- layer_out: bfloat16 [8192, 768], P('dp')
- grad_in: bfloat16 [8192, 768], P('dp')
- grad_qkv: float32 [3, 768, 768], P(None, None, 'tensor')
- grad_out: float32 [768, 768], P('tensor')
- grad_ff1: float32 [768, 768], P(None, 'tensor')
- grad_ff2: float32 [768, 768], P('tensor')
- grad_ln1_gain: float32 [768], replicated
- grad_ln1_bias: float32 [768], replicated
- grad_ln2_gain: float32 [768], replicated
- grad_ln2_bias: float32 [768], replicated
- grad_spd: float32 [32, 32], P(None, 'tensor')
- grad_edge: float32 [32, 32], P(None, 'tensor')
- grad_kernel_w1: float32 [128, 128], replicated
- grad_kernel_w2: float32 [128, 32], P(None, 'tensor')
- grad_centers: float32 [128], replicated
- grad_widths: float32 [128], replicated
Inputs may be any that keep to these rules, and one draw needn't show every extreme that they name: `atom_count`: every molecule has at least 16 real atoms, and some molecule has exactly 64.
All inputs are finite; a program needn't handle non-finite values.
Results may differ from a plain program's by a relative error of at most 0.02.
Values may be sent and summed in bfloat16 or wider, within the bound.
No kernel may reach another device: no remote copies, remote signals or barrier semaphores. Data moves between devices by JAX's collectives and lax.ppermute only.
A program may use at most 128 MiB of HBM per device.

v0:
```python
from functools import partial
import math
import jax
import jax.numpy as jnp
from jax import lax
from jax.sharding import PartitionSpec as P

DIST = 128
eps = 1e-05
neg_fill = -1000000000.0
highest = lax.Precision.HIGHEST


def norm_rows(values, gain, shift):
    center = values - jnp.mean(values, axis=-1, keepdims=True)
    spread = jnp.mean(center * center, axis=-1, keepdims=True)
    return center * lax.rsqrt(spread + eps) * gain + shift


def gelu_exact(values):
    return jax.nn.gelu(values, approximate=False)


def kernels(dist, centers, widths):
    place = dist.astype(jnp.float32)[..., None] * (8.0 / DIST)
    offset = (place - centers) / widths
    return jnp.exp(-0.5 * offset * offset) / widths


def kernel_geo(weights, dist_rows):
    kernel_w1, kernel_w2, centers, widths = weights
    total = dist_rows.shape[0]
    block = math.gcd(total, 16384)

    def one_block(rows):
        basis = kernels(rows, centers, widths).astype(jnp.bfloat16)
        inner = jnp.dot(basis, kernel_w1, preferred_element_type=jnp.float32)
        hidden = gelu_exact(inner).astype(jnp.bfloat16)
        return jnp.dot(hidden, kernel_w2, preferred_element_type=jnp.float32)

    result = lax.map(one_block, dist_rows.reshape(total // block, block))
    return result.reshape(total, kernel_w2.shape[1])


def kernel_grads(weights, dist_rows, grad_geo):
    kernel_w1, kernel_w2, centers, widths = weights
    total = dist_rows.shape[0]
    block = math.gcd(total, 16384)

    def one_block(carry, items):
        acc_one, acc_two, acc_center, acc_width = carry
        rows, grad_rows = items
        basis, basis_pull = jax.vjp(lambda cen, wid: kernels(rows, cen, wid), centers, widths)
        basis_b = basis.astype(jnp.bfloat16)
        inner = jnp.dot(basis_b, kernel_w1, preferred_element_type=jnp.float32)
        hidden, gelu_pull = jax.vjp(gelu_exact, inner)
        hidden_b = hidden.astype(jnp.bfloat16)
        acc_two = acc_two + jnp.dot(hidden_b.T, grad_rows, preferred_element_type=jnp.float32)
        grad_hidden = jnp.dot(grad_rows, kernel_w2.T, preferred_element_type=jnp.float32)
        grad_inner = gelu_pull(grad_hidden)[0].astype(jnp.bfloat16)
        acc_one = acc_one + jnp.dot(basis_b.T, grad_inner, preferred_element_type=jnp.float32)
        grad_basis = jnp.dot(grad_inner, kernel_w1.T, preferred_element_type=jnp.float32)
        grad_center, grad_width = basis_pull(grad_basis)
        return ((acc_one, acc_two, acc_center + grad_center, acc_width + grad_width), None)

    start_carry = (
        jnp.zeros(kernel_w1.shape, jnp.float32),
        jnp.zeros(kernel_w2.shape, jnp.float32),
        jnp.zeros(centers.shape, jnp.float32),
        jnp.zeros(widths.shape, jnp.float32),
    )
    result, unused = lax.scan(
        one_block,
        start_carry,
        (
            dist_rows.reshape(total // block, block),
            grad_geo.reshape(total // block, block, grad_geo.shape[1]),
        ),
    )
    return result


def block_bias(tables, mode, spd_ids, edge_ids, geo):
    spd_table, edge_table = tables
    spd_hot = jax.nn.one_hot(spd_ids, spd_table.shape[0], dtype=jnp.float32)
    edge_hot = jax.nn.one_hot(edge_ids, edge_table.shape[0], dtype=jnp.float32)
    flat = jnp.dot(spd_hot, spd_table, precision=highest) + jnp.dot(
        edge_hot, edge_table, precision=highest
    )
    two_flag = (mode != 1).astype(jnp.float32)[:, None, None, None]
    three_flag = (mode != 0).astype(jnp.float32)[:, None, None, None]
    return (two_flag * flat + three_flag * geo, spd_hot, edge_hot, two_flag, three_flag)


def scores_of(query, keyset, bias, count):
    atoms = query.shape[1]
    scores = jnp.einsum("bihe,bjhe->bhij", query, keyset, preferred_element_type=jnp.float32)
    scores = scores + jnp.transpose(bias, (0, 3, 1, 2))
    keep = (jnp.arange(atoms)[None, :] < count[:, None])[:, None, None, :]
    return jnp.where(keep, scores, neg_fill)


def attend(tables, items):
    query, keyset, values, count, mode, spd_ids, edge_ids, geo = items
    bias = block_bias(tables, mode, spd_ids, edge_ids, geo)[0]
    scores = scores_of(query, keyset, bias, count)
    row_max = jnp.max(scores, axis=-1, keepdims=True)
    expos = jnp.exp(scores - row_max)
    totals = jnp.sum(expos, axis=-1, keepdims=True)
    probs = (expos / totals).astype(jnp.bfloat16)
    mixed = jnp.einsum("bhij,bjhe->bihe", probs, values, preferred_element_type=jnp.float32)
    return (mixed.astype(jnp.bfloat16), row_max + jnp.log(totals))


def attend_back(tables, carry, items):
    query, keyset, values, grad_mixed, log_sums, count, mode, spd_ids, edge_ids, geo = items
    acc_spd, acc_edge = carry
    bias, spd_hot, edge_hot, two_flag, three_flag = block_bias(tables, mode, spd_ids, edge_ids, geo)
    scores = scores_of(query, keyset, bias, count)
    probs = jnp.exp(scores - log_sums)
    grad_values = jnp.einsum(
        "bhij,bihe->bjhe",
        probs.astype(jnp.bfloat16),
        grad_mixed,
        preferred_element_type=jnp.float32,
    )
    grad_probs = jnp.einsum(
        "bihe,bjhe->bhij", grad_mixed, values, preferred_element_type=jnp.float32
    )
    grad_scores = probs * (grad_probs - jnp.sum(probs * grad_probs, axis=-1, keepdims=True))
    grad_scores = grad_scores.astype(jnp.bfloat16)
    grad_query = jnp.einsum(
        "bhij,bjhe->bihe", grad_scores, keyset, preferred_element_type=jnp.float32
    )
    grad_keys = jnp.einsum(
        "bhij,bihe->bjhe", grad_scores, query, preferred_element_type=jnp.float32
    )
    grad_bias = jnp.transpose(grad_scores, (0, 2, 3, 1))
    flat_grad = two_flag.astype(jnp.bfloat16) * grad_bias
    acc_spd = acc_spd + jnp.einsum(
        "bijs,bijh->sh", spd_hot.astype(jnp.bfloat16), flat_grad, preferred_element_type=jnp.float32
    )
    acc_edge = acc_edge + jnp.einsum(
        "bijs,bijh->sh",
        edge_hot.astype(jnp.bfloat16),
        flat_grad,
        preferred_element_type=jnp.float32,
    )
    geo_grad = three_flag.astype(jnp.bfloat16) * grad_bias
    outputs = (
        grad_query.astype(jnp.bfloat16),
        grad_keys.astype(jnp.bfloat16),
        grad_values.astype(jnp.bfloat16),
        geo_grad,
    )
    return ((acc_spd, acc_edge), outputs)


def gain_grads(values, gain, shift, grad_rows):
    pull = jax.vjp(norm_rows, values, gain, shift)[1]
    return pull(grad_rows)


def body(
    hidden_in,
    w_qkv,
    w_out,
    w_ff1,
    w_ff2,
    ln1_gain,
    ln1_bias,
    ln2_gain,
    ln2_bias,
    spd_table,
    edge_table,
    kernel_w1,
    kernel_w2,
    centers,
    widths,
    atom_count,
    mol_mode,
    spd_bucket,
    edge_type,
    dist_bucket,
    cotangent,
):
    tokens = hidden_in.shape[0]
    mols, atoms = (spd_bucket.shape[0], spd_bucket.shape[1])
    heads_here = spd_table.shape[1]
    columns = w_qkv.shape[2]
    head_dim = columns // heads_here
    group = math.gcd(mols, max(1, 2048 // atoms))
    count_blocks = mols // group
    scale = 1.0 / math.sqrt(head_dim)
    tables = (spd_table, edge_table)
    pairs = mols * atoms * atoms
    dist_rows = dist_bucket.reshape(pairs)

    def by_block(array):
        return array.reshape((count_blocks, group) + array.shape[1:])

    def heads_view(array):
        return array.reshape(count_blocks, group, atoms, heads_here, head_dim)

    source = hidden_in.astype(jnp.float32)
    upstream = cotangent.astype(jnp.float32)
    share_rows = tokens // lax.axis_size("tensor")
    start = lax.axis_index("tensor") * share_rows
    source_share = lax.dynamic_slice_in_dim(source, start, share_rows, 0)
    geo = kernel_geo((kernel_w1, kernel_w2, centers, widths), dist_rows)
    geo_view = geo.reshape(count_blocks, group, atoms, atoms, heads_here)
    normed_one = norm_rows(source, ln1_gain, ln1_bias).astype(jnp.bfloat16)
    projected = jnp.einsum("td,kdc->ktc", normed_one, w_qkv, preferred_element_type=jnp.float32)
    query_b = (projected[0] * scale).astype(jnp.bfloat16)
    key_b = projected[1].astype(jnp.bfloat16)
    value_b = projected[2].astype(jnp.bfloat16)
    int_items = (
        by_block(atom_count),
        by_block(mol_mode),
        by_block(spd_bucket),
        by_block(edge_type),
        geo_view,
    )
    attended, log_sums = lax.map(
        partial(attend, tables),
        (heads_view(query_b), heads_view(key_b), heads_view(value_b)) + int_items,
    )
    attended = attended.reshape(tokens, columns)
    attn_part = jnp.dot(attended, w_out, preferred_element_type=jnp.float32)
    middle = source + lax.psum(attn_part.astype(jnp.bfloat16), "tensor").astype(jnp.float32)
    normed_two = norm_rows(middle, ln2_gain, ln2_bias).astype(jnp.bfloat16)
    inner = jnp.dot(normed_two, w_ff1, preferred_element_type=jnp.float32)
    active = gelu_exact(inner).astype(jnp.bfloat16)
    ffn_part = jnp.dot(active, w_ff2, preferred_element_type=jnp.float32)
    layer_out = (
        middle + lax.psum(ffn_part.astype(jnp.bfloat16), "tensor").astype(jnp.float32)
    ).astype(jnp.bfloat16)
    grad_ff2 = jnp.dot(active.T, cotangent, preferred_element_type=jnp.float32)
    grad_active = jnp.dot(cotangent, w_ff2.T, preferred_element_type=jnp.float32)
    gelu_pull = jax.vjp(gelu_exact, inner)[1]
    grad_inner = gelu_pull(grad_active)[0].astype(jnp.bfloat16)
    grad_ff1 = jnp.dot(normed_two.T, grad_inner, preferred_element_type=jnp.float32)
    two_part = jnp.dot(grad_inner, w_ff1.T, preferred_element_type=jnp.float32)
    two_grad = lax.psum(two_part.astype(jnp.bfloat16), "tensor").astype(jnp.float32)
    back_middle = gain_grads(middle, ln2_gain, ln2_bias, two_grad)[0]
    middle_share = lax.dynamic_slice_in_dim(middle, start, share_rows, 0)
    two_share = lax.dynamic_slice_in_dim(two_grad, start, share_rows, 0)
    unused, grad_g2, grad_b2 = gain_grads(middle_share, ln2_gain, ln2_bias, two_share)
    middle_grad = upstream + back_middle
    middle_grad_b = middle_grad.astype(jnp.bfloat16)
    grad_out = jnp.dot(attended.T, middle_grad_b, preferred_element_type=jnp.float32)
    grad_attended = jnp.dot(middle_grad_b, w_out.T, preferred_element_type=jnp.float32).astype(
        jnp.bfloat16
    )
    carry_start = (
        jnp.zeros(spd_table.shape, jnp.float32),
        jnp.zeros(edge_table.shape, jnp.float32),
    )
    table_grads, back_outs = lax.scan(
        partial(attend_back, tables),
        carry_start,
        (
            heads_view(query_b),
            heads_view(key_b),
            heads_view(value_b),
            heads_view(grad_attended),
            log_sums,
        )
        + int_items,
    )
    grad_spd, grad_edge = table_grads
    geo_grad = back_outs[3].reshape(pairs, heads_here)
    grad_kw1, grad_kw2, grad_cen, grad_wid = kernel_grads(
        (kernel_w1, kernel_w2, centers, widths), dist_rows, geo_grad
    )
    grad_qkv_b = jnp.stack(
        [
            back_outs[0].reshape(tokens, columns),
            back_outs[1].reshape(tokens, columns),
            back_outs[2].reshape(tokens, columns),
        ]
    )
    factor = jnp.array([scale, 1.0, 1.0], jnp.float32)[:, None, None]
    grad_qkv = (
        jnp.einsum("td,ktc->kdc", normed_one, grad_qkv_b, preferred_element_type=jnp.float32)
        * factor
    )
    one_parts = jnp.einsum("ktc,kdc->ktd", grad_qkv_b, w_qkv, preferred_element_type=jnp.float32)
    one_part = jnp.sum(one_parts * factor, axis=0)
    one_grad = lax.psum(one_part.astype(jnp.bfloat16), "tensor").astype(jnp.float32)
    back_source = gain_grads(source, ln1_gain, ln1_bias, one_grad)[0]
    one_share = lax.dynamic_slice_in_dim(one_grad, start, share_rows, 0)
    unused, grad_g1, grad_b1 = gain_grads(source_share, ln1_gain, ln1_bias, one_share)
    grad_in = (middle_grad + back_source).astype(jnp.bfloat16)
    sharded = (
        lax.psum(grad_qkv.astype(jnp.bfloat16), "dp").astype(jnp.float32),
        lax.psum(grad_out.astype(jnp.bfloat16), "dp").astype(jnp.float32),
        lax.psum(grad_ff1.astype(jnp.bfloat16), "dp").astype(jnp.float32),
        lax.psum(grad_ff2.astype(jnp.bfloat16), "dp").astype(jnp.float32),
        lax.psum(grad_spd.astype(jnp.bfloat16), "dp").astype(jnp.float32),
        lax.psum(grad_edge.astype(jnp.bfloat16), "dp").astype(jnp.float32),
        lax.psum(grad_kw2.astype(jnp.bfloat16), "dp").astype(jnp.float32),
    )
    shared = lax.psum(
        (grad_kw1, grad_cen, grad_wid, grad_g1, grad_b1, grad_g2, grad_b2), ("dp", "tensor")
    )
    return (
        layer_out,
        grad_in,
        sharded[0],
        sharded[1],
        sharded[2],
        sharded[3],
        shared[3],
        shared[4],
        shared[5],
        shared[6],
        sharded[4],
        sharded[5],
        shared[0],
        sharded[6],
        shared[1],
        shared[2],
    )


def solution(mesh):
    in_specs = (
        P("dp", None),
        P(None, None, "tensor"),
        P("tensor", None),
        P(None, "tensor"),
        P("tensor", None),
        P(),
        P(),
        P(),
        P(),
        P(None, "tensor"),
        P(None, "tensor"),
        P(),
        P(None, "tensor"),
        P(),
        P(),
        P("dp"),
        P("dp"),
        P("dp", None, None),
        P("dp", None, None),
        P("dp", None, None),
        P("dp", None),
    )
    out_specs = (
        P("dp", None),
        P("dp", None),
        P(None, None, "tensor"),
        P("tensor", None),
        P(None, "tensor"),
        P("tensor", None),
        P(),
        P(),
        P(),
        P(),
        P(None, "tensor"),
        P(None, "tensor"),
        P(),
        P(None, "tensor"),
        P(),
        P(),
    )
    return jax.shard_map(body, mesh=mesh, in_specs=in_specs, out_specs=out_specs, check_vma=False)
```

profile of v0, /device:TPU:1, one launch (start us, length us, event | category | flops | bytes accessed | tf_op | source)
XLA Modules:
  0.0 702.5 jit_solution(9813940309770022953)
XLA Ops:
  17.9 129.2 %while.6 = (s32[]{:T(128)}, f32[4,16384,8]{1,0,2:T(4,128)}, s32[4,16384]{1,0:T(4,128)S(1)}, f32[128]{0:T(128)S(1)}, f32[128]{0:T(128)S(1)}, /*index=5*/bf16[128,...) while((s32[]{:T(128)}, f32[4,16384,8]{1,0,2:T(4,128)}, s32[4,16384]{1,0:T(4,128)S(1)}, ...), condition=%wide.region_3.4_spmd, body=%wide.region_2.3_spmd.sunk | while | flops 719355904 | bytes 2853997 | solution.py:41
  18.2 21.2 %convolution_bitcast_fusion.2 = f32[1,16384,8]{1,2,0:T(8,128)S(1)} fusion(bf16[128,8]{0,1:T(8,128)(2,1)S(1)} %get-tuple-element.560, bf16[128,128]{1,0:T(8,128)(2,1)S(1)} %get-tuple-element.559, f32[128]{0:T(128)S(1)} %get-tuple-element.558, f32[128]{0:T(128)S(1)} %get-tuple-element.557, f32[16384]{0:T(1024)S(1)} %bitcast.180), kind=kOutput, calls=%fused_computation.clone.1 | convolution fusion | flops 719323136 | bytes 625664 | tf_op jit(solution)/shard_map/while/body/eval_jaxpr/dot_general | solution.py:39
  39.9 10.5 %dynamic_update_slice.20 = f32[4,16384,8]{1,0,2:T(4,128)} dynamic-update-slice(f32[4,16384,8]{1,0,2:T(4,128)} %get-tuple-element.546, f32[1,16384,8]{1,0,2:T(1,128)S(1)} %copy.132, s32[]{:T(128)S(6)} %copy.136, s32[]{:T(128)} %constant.311.clone.1..sunk, s32[]{:T(128)} %constant.311.clone.1..sunk) | dynamic-update-slice | bytes 1048580 | tf_op jit(solution)/shard_map/while/body/jit(dynamic_update_index_in_dim)/dynamic_update_slice | solution.py:41
  50.4 21.2 %convolution_bitcast_fusion.2 = f32[1,16384,8]{1,2,0:T(8,128)S(1)} fusion(bf16[128,8]{0,1:T(8,128)(2,1)S(1)} %get-tuple-element.560, bf16[128,128]{1,0:T(8,128)(2,1)S(1)} %get-tuple-element.559, f32[128]{0:T(128)S(1)} %get-tuple-element.558, f32[128]{0:T(128)S(1)} %get-tuple-element.557, f32[16384]{0:T(1024)S(1)} %bitcast.180), kind=kOutput, calls=%fused_computation.clone.1 | convolution fusion | flops 719323136 | bytes 625664 | tf_op jit(solution)/shard_map/while/body/eval_jaxpr/dot_general | solution.py:39
  72.2 10.5 %dynamic_update_slice.20 = f32[4,16384,8]{1,0,2:T(4,128)} dynamic-update-slice(f32[4,16384,8]{1,0,2:T(4,128)} %get-tuple-element.546, f32[1,16384,8]{1,0,2:T(1,128)S(1)} %copy.132, s32[]{:T(128)S(6)} %copy.136, s32[]{:T(128)} %constant.311.clone.1..sunk, s32[]{:T(128)} %constant.311.clone.1..sunk) | dynamic-update-slice | bytes 1048580 | tf_op jit(solution)/shard_map/while/body/jit(dynamic_update_index_in_dim)/dynamic_update_slice | solution.py:41
  82.7 21.2 %convolution_bitcast_fusion.2 = f32[1,16384,8]{1,2,0:T(8,128)S(1)} fusion(bf16[128,8]{0,1:T(8,128)(2,1)S(1)} %get-tuple-element.560, bf16[128,128]{1,0:T(8,128)(2,1)S(1)} %get-tuple-element.559, f32[128]{0:T(128)S(1)} %get-tuple-element.558, f32[128]{0:T(128)S(1)} %get-tuple-element.557, f32[16384]{0:T(1024)S(1)} %bitcast.180), kind=kOutput, calls=%fused_computation.clone.1 | convolution fusion | flops 719323136 | bytes 625664 | tf_op jit(solution)/shard_map/while/body/eval_jaxpr/dot_general | solution.py:39
  104.4 10.5 %dynamic_update_slice.20 = f32[4,16384,8]{1,0,2:T(4,128)} dynamic-update-slice(f32[4,16384,8]{1,0,2:T(4,128)} %get-tuple-element.546, f32[1,16384,8]{1,0,2:T(1,128)S(1)} %copy.132, s32[]{:T(128)S(6)} %copy.136, s32[]{:T(128)} %constant.311.clone.1..sunk, s32[]{:T(128)} %constant.311.clone.1..sunk) | dynamic-update-slice | bytes 1048580 | tf_op jit(solution)/shard_map/while/body/jit(dynamic_update_index_in_dim)/dynamic_update_slice | solution.py:41
  115.0 21.2 %convolution_bitcast_fusion.2 = f32[1,16384,8]{1,2,0:T(8,128)S(1)} fusion(bf16[128,8]{0,1:T(8,128)(2,1)S(1)} %get-tuple-element.560, bf16[128,128]{1,0:T(8,128)(2,1)S(1)} %get-tuple-element.559, f32[128]{0:T(128)S(1)} %get-tuple-element.558, f32[128]{0:T(128)S(1)} %get-tuple-element.557, f32[16384]{0:T(1024)S(1)} %bitcast.180), kind=kOutput, calls=%fused_computation.clone.1 | convolution fusion | flops 719323136 | bytes 625664 | tf_op jit(solution)/shard_map/while/body/eval_jaxpr/dot_general | solution.py:39
  136.7 10.5 %dynamic_update_slice.20 = f32[4,16384,8]{1,0,2:T(4,128)} dynamic-update-slice(f32[4,16384,8]{1,0,2:T(4,128)} %get-tuple-element.546, f32[1,16384,8]{1,0,2:T(1,128)S(1)} %copy.132, s32[]{:T(128)S(6)} %copy.136, s32[]{:T(128)} %constant.311.clone.1..sunk, s32[]{:T(128)} %constant.311.clone.1..sunk) | dynamic-update-slice | bytes 1048580 | tf_op jit(solution)/shard_map/while/body/jit(dynamic_update_index_in_dim)/dynamic_update_slice | solution.py:41
  147.9 5.0 squeeze.56
  152.9 5.5 copy.59
  163.3 7.7 %fusion.83 = f32[16,64,64,8]{2,3,1,0:T(8,128)} fusion(s32[16,64,64]{2,1,0:T(8,128)} %param.43, f32[32,8]{0,1:T(8,128)S(1)} %copy-done.68), kind=kOutput, calls=%fused_computation.114 | convolution fusion | flops 203423744 | bytes 2360320 | tf_op jit(solution)/shard_map/while/body/eval_jaxpr/dot_general | solution.py:87
  171.0 5.4 copy.56
  176.4 7.5 %fusion.82 = f32[16,64,64,8]{2,3,1,0:T(8,128)} fusion(s32[16,64,64]{2,1,0:T(8,128)} %param.44, f32[32,8]{0,1:T(8,128)S(1)} %copy-done.69), kind=kOutput, calls=%fused_computation.112 | convolution fusion | flops 203423744 | bytes 2360320 | tf_op jit(solution)/shard_map/while/body/eval_jaxpr/dot_general | solution.py:87
  183.9 5.4 copy.57
  189.3 8.2 %fusion.153 = (f32[16,8,64]{2,1,0:T(8,128)S(1)}, f32[16,8,64,64]{2,3,1,0:T(8,128)S(1)}, f32[16,64,64,8]{1,2,3,0:T(8,128)}, f32[16,8,64,64]{2,3,1,0:T(8,128)}) fusion(pred[16,64]{1,0:T(8,128)(4,1)S(1)} %copy-done.61, f32[16,64,64,8]{1,2,3,0:T(8,128)} %copy.59, f32[16]{0:T(128)S(1)} %copy-done.75, f32[16,64,64,8]{1,2,3,0:T(8,128)} %copy.56, ...), kind=kOutput, calls=%fused_computation.248 | convolution fusion | flops 28827648 | bytes 13403264 | tf_op jit(solution)/shard_map/while/body/eval_jaxpr/bihe,bjhe->bhij/dot_general | solution.py:97
  211.7 39.8 %all-reduce.10.cloned.1.call-done = bf16[1024,768]{1,0:T(8,128)(2,1)} async-done(((bf16[1024,768]{1,0:T(8,128)(2,1)}), bf16[1024,768]{1,0:T(8,128)(2,1)}) %all-reduce.10.cloned.1.call-update) | async-done | bytes 1572880 | tf_op jit(solution)/shard_map/psum | solution.py:230
  251.5 3.6 convert_add_fusion
  274.6 36.9 %all-reduce.12.cloned.1.call-done = bf16[1024,768]{1,0:T(8,128)(2,1)} async-done(((bf16[1024,768]{1,0:T(8,128)(2,1)}), bf16[1024,768]{1,0:T(8,128)(2,1)}) %all-reduce.12.cloned.1.call-update) | async-done | bytes 1572880 | tf_op jit(solution)/shard_map/psum | solution.py:244
  323.6 3.8 fusion.116
  353.1 6.6 broadcast_multiply_fusion.1
  361.3 4.0 copy.76
  365.4 3.6 reshape_reshape.9
  375.6 165.0 %while.7 = (s32[]{:T(128)}, f32[128,128]{1,0:T(8,128)S(1)}, f32[128,8]{0,1:T(8,128)S(1)}, f32[128]{0:T(128)}, f32[128]{0:T(128)}, /*index=5*/s32[4,16384]{1,0:T(...) while((s32[]{:T(128)}, f32[128,128]{1,0:T(8,128)S(1)}, ...), condition=%wide.region_40.41_spmd.clone, body=%wide.region_36.40_spmd.clone.sunk | while | flops 1914768128 | bytes 101811056 | solution.py:72
  376.8 19.5 %fusion.218 = (f32[16384,128]{1,0:T(8,128)S(1)}, f32[16384,128]{1,0:T(8,128)S(1)}) fusion(bf16[128,128]{1,0:T(8,128)(2,1)S(1)} %get-tuple-element.599, f32[128]{0:T(128)S(1)} %get-tuple-element.598, f32[128]{0:T(128)S(1)} %get-tuple-element.597, f32[16384]{0:T(1024)S(1)} %bitcast.173), kind=kOutput, calls=%fused_computation.69.clone.1 | convolution fusion | flops 679477248 | bytes 16876544 | tf_op jit(solution)/shard_map/while/body/eval_jaxpr/dot_general | solution.py:55
  397.1 4.3 add_convert_fusion.9
  401.5 3.8 fusion.219
  405.3 3.6 fusion.221
  408.9 7.4 %fusion.222 = (f32[128]{0:T(128)S(1)}, f32[128]{0:T(128)S(1)}, f32[128]{0:T(128)S(1)}) fusion(f32[16384,128]{1,0:T(8,128)S(1)} %get-tuple-element.529, f32[128]{0:T(128)S(1)} %divide_bitcast_fusion.2, f32[128]{0:T(128)S(1)} %get-tuple-element.597, f32[16384]{0:T(1024)S(1)} %bitcast.176, f32[128]{0:T(128)S(1)} %get-tuple-element.598, ...), kind=kLoop, calls=%fused_computation.66.clone.1 | loop fusion | flops 25165440 | bytes 16845824 | tf_op jit(solution)/shard_map/while/body/eval_jaxpr/transpose(jvp())/reduce_sum | solution.py:26
  418.0 19.5 %fusion.218 = (f32[16384,128]{1,0:T(8,128)S(1)}, f32[16384,128]{1,0:T(8,128)S(1)}) fusion(bf16[128,128]{1,0:T(8,128)(2,1)S(1)} %get-tuple-element.599, f32[128]{0:T(128)S(1)} %get-tuple-element.598, f32[128]{0:T(128)S(1)} %get-tuple-element.597, f32[16384]{0:T(1024)S(1)} %bitcast.173), kind=kOutput, calls=%fused_computation.69.clone.1 | convolution fusion | flops 679477248 | bytes 16876544 | tf_op jit(solution)/shard_map/while/body/eval_jaxpr/dot_general | solution.py:55
  438.3 4.3 add_convert_fusion.9
  442.6 3.8 fusion.219
  446.4 3.6 fusion.221
  450.1 7.4 %fusion.222 = (f32[128]{0:T(128)S(1)}, f32[128]{0:T(128)S(1)}, f32[128]{0:T(128)S(1)}) fusion(f32[16384,128]{1,0:T(8,128)S(1)} %get-tuple-element.529, f32[128]{0:T(128)S(1)} %divide_bitcast_fusion.2, f32[128]{0:T(128)S(1)} %get-tuple-element.597, f32[16384]{0:T(1024)S(1)} %bitcast.176, f32[128]{0:T(128)S(1)} %get-tuple-element.598, ...), kind=kLoop, calls=%fused_computation.66.clone.1 | loop fusion | flops 25165440 | bytes 16845824 | tf_op jit(solution)/shard_map/while/body/eval_jaxpr/transpose(jvp())/reduce_sum | solution.py:26
  459.1 19.5 %fusion.218 = (f32[16384,128]{1,0:T(8,128)S(1)}, f32[16384,128]{1,0:T(8,128)S(1)}) fusion(bf16[128,128]{1,0:T(8,128)(2,1)S(1)} %get-tuple-element.599, f32[128]{0:T(128)S(1)} %get-tuple-element.598, f32[128]{0:T(128)S(1)} %get-tuple-element.597, f32[16384]{0:T(1024)S(1)} %bitcast.173), kind=kOutput, calls=%fused_computation.69.clone.1 | convolution fusion | flops 679477248 | bytes 16876544 | tf_op jit(solution)/shard_map/while/body/eval_jaxpr/dot_general | solution.py:55
  479.5 4.3 add_convert_fusion.9
  483.8 3.8 fusion.219
  487.6 3.6 fusion.221
  491.2 7.4 %fusion.222 = (f32[128]{0:T(128)S(1)}, f32[128]{0:T(128)S(1)}, f32[128]{0:T(128)S(1)}) fusion(f32[16384,128]{1,0:T(8,128)S(1)} %get-tuple-element.529, f32[128]{0:T(128)S(1)} %divide_bitcast_fusion.2, f32[128]{0:T(128)S(1)} %get-tuple-element.597, f32[16384]{0:T(1024)S(1)} %bitcast.176, f32[128]{0:T(128)S(1)} %get-tuple-element.598, ...), kind=kLoop, calls=%fused_computation.66.clone.1 | loop fusion | flops 25165440 | bytes 16845824 | tf_op jit(solution)/shard_map/while/body/eval_jaxpr/transpose(jvp())/reduce_sum | solution.py:26
  500.3 19.5 %fusion.218 = (f32[16384,128]{1,0:T(8,128)S(1)}, f32[16384,128]{1,0:T(8,128)S(1)}) fusion(bf16[128,128]{1,0:T(8,128)(2,1)S(1)} %get-tuple-element.599, f32[128]{0:T(128)S(1)} %get-tuple-element.598, f32[128]{0:T(128)S(1)} %get-tuple-element.597, f32[16384]{0:T(1024)S(1)} %bitcast.173), kind=kOutput, calls=%fused_computation.69.clone.1 | convolution fusion | flops 679477248 | bytes 16876544 | tf_op jit(solution)/shard_map/while/body/eval_jaxpr/dot_general | solution.py:55
  520.6 4.3 add_convert_fusion.9
  525.0 3.8 fusion.219
  528.7 3.6 fusion.221
  532.4 7.4 %fusion.222 = (f32[128]{0:T(128)S(1)}, f32[128]{0:T(128)S(1)}, f32[128]{0:T(128)S(1)}) fusion(f32[16384,128]{1,0:T(8,128)S(1)} %get-tuple-element.529, f32[128]{0:T(128)S(1)} %divide_bitcast_fusion.2, f32[128]{0:T(128)S(1)} %get-tuple-element.597, f32[16384]{0:T(1024)S(1)} %bitcast.176, f32[128]{0:T(128)S(1)} %get-tuple-element.598, ...), kind=kLoop, calls=%fused_computation.66.clone.1 | loop fusion | flops 25165440 | bytes 16845824 | tf_op jit(solution)/shard_map/while/body/eval_jaxpr/transpose(jvp())/reduce_sum | solution.py:26
  543.5 4.0 fusion.123
  549.8 18.0 %all-reduce.1 = (bf16[32,8]{0,1:T(8,128)(2,1)S(1)}, bf16[32,8]{0,1:T(8,128)(2,1)S(1)}, bf16[128,8]{0,1:T(8,128)(2,1)S(1)}) all-reduce(bf16[32,8]{0,1:T(8,128)(2,1)S(1)} %fusion.122, bf16[32,8]{0,1:T(8,128)(2,1)S(1)} %fusion.123, bf16[128,8]{0,1:T(8,128)(2,1)S(1)} %convert_element_type.292), channel_id=1, replica_groups=mesh['dp'=8,'tensor'=4] {'dp'}, use_global_device_ids=true, to_apply=%region_34.35 | all-reduce | flops 1536 | bytes 6144 | tf_op jit(solution)/shard_map/psum | solution.py:300
  582.9 40.9 %all-reduce = (f32[768]{0:T(1024)}, f32[768]{0:T(1024)}, f32[768]{0:T(1024)}, f32[768]{0:T(1024)}, f32[128]{0:T(128)}, /*index=5*/f32[128]{0:T(128)}) all-reduce(f32[768]{0:T(1024)S(1)} %get-tuple-element.320, f32[768]{0:T(1024)S(1)} %get-tuple-element.319, ...), channel_id=1, replica_groups=mesh['dp'=8,'tensor'=4] {'dp','tensor'}, use_global_device_ids=true, to_apply=%region_25.26 | all-reduce | flops 3328 | bytes 26624 | tf_op jit(solution)/shard_map/psum | solution.py:304
  631.8 62.5 %all-reduce.14.cloned.1.call-done = f32[128,128]{1,0:T(8,128)} async-done(((f32[128,128]{1,0:T(8,128)}), f32[128,128]{1,0:T(8,128)}) %all-reduce.14.cloned.1.call-update) | async-done | bytes 65552 | tf_op jit(solution)/shard_map/psum | solution.py:304
  (343 shorter events, 137.5 us)
Async XLA Ops:
  7.2 244.3 %all-reduce.10.cloned.1.call-start = ((), (), s32[]{:S(2)}) async-start(), calls=%async_computation | async-start | bytes 3145728 | tf_op jit(solution)/shard_map/psum | solution.py:230
  159.7 39.1 %copy-start.26 = (bf16[16,64,8,24]{1,0,3,2:T(8,128)(2,1)}, bf16[16,64,8,24]{1,0,3,2:T(8,128)(2,1)S(1)}, u32[]{:S(2)}) copy-start(bf16[16,64,8,24]{1,0,3,2:T(8,128)(2,1)S(1)} %convert_element_type.239) | copy-start | bytes 1179652
  163.3 26.0 %copy-start.18 = (bf16[16,64,8,24]{1,0,3,2:T(8,128)(2,1)}, bf16[16,64,8,24]{1,0,3,2:T(8,128)(2,1)S(1)}, u32[]{:S(2)}) copy-start(bf16[16,64,8,24]{1,0,3,2:T(8,128)(2,1)S(1)} %convert_element_type.242) | copy-start | bytes 1179652
  199.9 6.8 copy-start.2
  206.6 105.0 %all-reduce.12.cloned.1.call-start = ((), (), s32[]{:S(2)}) async-start(), calls=%async_computation.1 | async-start | bytes 3145728 | tf_op jit(solution)/shard_map/psum | solution.py:244
  209.8 46.1 %copy-start.64 = (f32[256]{0:T(256)}, f32[256]{0:T(256)S(1)}, u32[]{:S(2)}) copy-start(f32[256]{0:T(256)S(1)} %broadcast_multiply_fusion.5) | copy-start | bytes 3076
  211.7 44.2 %copy-start.45 = (f32[768]{0:T(1024)S(1)}, f32[768]{0:T(1024)}, u32[]{:S(2)}) copy-start(f32[768]{0:T(1024)} %param.33) | copy-start | bytes 9220
  211.7 44.2 %copy-start.70 = (f32[768]{0:T(1024)S(1)}, f32[768]{0:T(1024)}, u32[]{:S(2)}) copy-start(f32[768]{0:T(1024)} %param.34) | copy-start | bytes 9220
  264.8 9.8 %copy-start.66 = (f32[256]{0:T(256)}, f32[256]{0:T(256)S(1)}, u32[]{:S(2)}) copy-start(f32[256]{0:T(256)S(1)} %broadcast_multiply_fusion.4) | copy-start | bytes 3076
  268.4 304.2 %all-reduce.18.cloned.1.call-start = ((), (), s32[]{:S(2)}) async-start(), calls=%async_computation.4 | async-start | bytes 6291456 | tf_op jit(solution)/shard_map/psum | solution.py:236
  333.2 10.3 %copy-start.28 = (bf16[16,64,8,24]{1,3,2,0:T(8,128)(2,1)S(1)}, bf16[16,64,8,24]{1,3,2,0:T(8,128)(2,1)}, u32[]{:S(2)}) copy-start(bf16[16,64,8,24]{1,3,2,0:T(8,128)(2,1)} %fusion.115) | copy-start | bytes 1179652
  338.6 11.7 %copy-start.85 = (f32[3]{0:T(128)S(1)}, f32[3]{0:T(128)}, u32[]{:S(2)}) copy-start(f32[3]{0:T(128)} %constant.348.clone) | copy-start | bytes 40
  353.0 270.7 %all-reduce.16.cloned.1.call-start = ((), (), s32[]{:S(2)}) async-start(), calls=%async_computation.3 | async-start | bytes 3538944 | tf_op jit(solution)/shard_map/psum | solution.py:296
  361.3 9.2 %copy-start.23 = (bf16[1024,192]{0,1:T(8,128)(2,1)S(1)}, bf16[1024,192]{0,1:T(8,128)(2,1)}, u32[]{:S(2)}) copy-start(bf16[1024,192]{0,1:T(8,128)(2,1)} %reshape.250) | copy-start | bytes 1179652
  365.3 7.8 %copy-start.41 = (f32[1024]{0:T(1024)S(1)}, f32[1024]{0:T(1024)}, u32[]{:S(2)}) copy-start(f32[1024]{0:T(1024)} %copy-done.40) | copy-start | bytes 12292
  365.3 7.8 %copy-start.48 = (f32[768]{0:T(1024)S(1)}, f32[768]{0:T(1024)}, u32[]{:S(2)}) copy-start(f32[768]{0:T(1024)} %param.31) | copy-start | bytes 9220
  365.3 7.8 %copy-start.51 = (f32[1024]{0:T(1024)S(1)}, f32[1024]{0:T(1024)}, u32[]{:S(2)}) copy-start(f32[1024]{0:T(1024)} %copy-done.50) | copy-start | bytes 12292
  365.3 7.8 %copy-start.80 = (f32[768]{0:T(1024)S(1)}, f32[768]{0:T(1024)}, u32[]{:S(2)}) copy-start(f32[768]{0:T(1024)} %param.32) | copy-start | bytes 9220
  365.3 7.8 %copy-start.86 = (f32[3]{0:T(128)S(1)}, f32[3]{0:T(128)}, u32[]{:S(2)}) copy-start(f32[3]{0:T(128)} %constant.348.clone) | copy-start | bytes 40
  375.5 318.8 %all-reduce.14.cloned.1.call-start = ((), (), s32[]{:S(2)}) async-start(), calls=%async_computation.2 | async-start | bytes 131072 | tf_op jit(solution)/shard_map/psum | solution.py:304
  375.6 165.0 %copy-start.17 = (bf16[16,64,64,8]{1,2,3,0:T(8,128)(2,1)S(1)}, bf16[16,64,64,8]{1,2,3,0:T(8,128)(2,1)}, u32[]{:S(2)}) copy-start(bf16[16,64,64,8]{1,2,3,0:T(8,128)(2,1)} %get-tuple-element.374) | copy-start | bytes 3145732
  375.6 20.7 %copy-start.83 = (f32[1,128]{1,0:T(1,128)}, f32[1,128]{1,0:T(1,128)S(1)}, u32[]{:S(2)}) copy-start(f32[1,128]{1,0:T(1,128)S(1)} %get-tuple-element.602) | copy-start | bytes 1540 | tf_op jit(solution)/shard_map/while
  376.8 19.5 %copy-start.22 = (bf16[4,16384,8]{1,2,0:T(8,128)(2,1)S(1)}, bf16[4,16384,8]{1,2,0:T(8,128)(2,1)}, u32[]{:S(2)}) copy-start(bf16[4,16384,8]{1,2,0:T(8,128)(2,1)} %get-tuple-element.600) | copy-start | bytes 3145732 | tf_op jit(solution)/shard_map/while
  408.9 7.4 %copy-start.55 = (f32[128]{0:T(128)S(1)}, f32[128]{0:T(128)}, u32[]{:S(2)}) copy-start(f32[128]{0:T(128)} %get-tuple-element.581) | copy-start | bytes 1540 | tf_op jit(solution)/shard_map/while
  408.9 7.4 %copy-start.58 = (f32[128]{0:T(128)S(1)}, f32[128]{0:T(128)}, u32[]{:S(2)}) copy-start(f32[128]{0:T(128)} %get-tuple-element.580) | copy-start | bytes 1540 | tf_op jit(solution)/shard_map/while
  408.9 8.0 %copy-start.84 = (f32[1,128]{1,0:T(1,128)S(1)}, f32[1,128]{1,0:T(1,128)}, u32[]{:S(2)}) copy-start(f32[1,128]{1,0:T(1,128)} %copy-done.83) | copy-start | bytes 1540 | tf_op jit(solution)/shard_map/while
  416.9 20.5 %copy-start.83 = (f32[1,128]{1,0:T(1,128)}, f32[1,128]{1,0:T(1,128)S(1)}, u32[]{:S(2)}) copy-start(f32[1,128]{1,0:T(1,128)S(1)} %get-tuple-element.602) | copy-start | bytes 1540 | tf_op jit(solution)/shard_map/while
  418.0 19.5 %copy-start.22 = (bf16[4,16384,8]{1,2,0:T(8,128)(2,1)S(1)}, bf16[4,16384,8]{1,2,0:T(8,128)(2,1)}, u32[]{:S(2)}) copy-start(bf16[4,16384,8]{1,2,0:T(8,128)(2,1)} %get-tuple-element.600) | copy-start | bytes 3145732 | tf_op jit(solution)/shard_map/while
  450.0 7.4 %copy-start.55 = (f32[128]{0:T(128)S(1)}, f32[128]{0:T(128)}, u32[]{:S(2)}) copy-start(f32[128]{0:T(128)} %get-tuple-element.581) | copy-start | bytes 1540 | tf_op jit(solution)/shard_map/while
  450.0 7.4 %copy-start.58 = (f32[128]{0:T(128)S(1)}, f32[128]{0:T(128)}, u32[]{:S(2)}) copy-start(f32[128]{0:T(128)} %get-tuple-element.580) | copy-start | bytes 1540 | tf_op jit(solution)/shard_map/while
  450.0 8.0 %copy-start.84 = (f32[1,128]{1,0:T(1,128)S(1)}, f32[1,128]{1,0:T(1,128)}, u32[]{:S(2)}) copy-start(f32[1,128]{1,0:T(1,128)} %copy-done.83) | copy-start | bytes 1540 | tf_op jit(solution)/shard_map/while
  458.1 20.5 %copy-start.83 = (f32[1,128]{1,0:T(1,128)}, f32[1,128]{1,0:T(1,128)S(1)}, u32[]{:S(2)}) copy-start(f32[1,128]{1,0:T(1,128)S(1)} %get-tuple-element.602) | copy-start | bytes 1540 | tf_op jit(solution)/shard_map/while
  459.1 19.5 %copy-start.22 = (bf16[4,16384,8]{1,2,0:T(8,128)(2,1)S(1)}, bf16[4,16384,8]{1,2,0:T(8,128)(2,1)}, u32[]{:S(2)}) copy-start(bf16[4,16384,8]{1,2,0:T(8,128)(2,1)} %get-tuple-element.600) | copy-start | bytes 3145732 | tf_op jit(solution)/shard_map/while
  491.2 7.4 %copy-start.55 = (f32[128]{0:T(128)S(1)}, f32[128]{0:T(128)}, u32[]{:S(2)}) copy-start(f32[128]{0:T(128)} %get-tuple-element.581) | copy-start | bytes 1540 | tf_op jit(solution)/shard_map/while
  491.2 7.4 %copy-start.58 = (f32[128]{0:T(128)S(1)}, f32[128]{0:T(128)}, u32[]{:S(2)}) copy-start(f32[128]{0:T(128)} %get-tuple-element.580) | copy-start | bytes 1540 | tf_op jit(solution)/shard_map/while
  491.2 8.0 %copy-start.84 = (f32[1,128]{1,0:T(1,128)S(1)}, f32[1,128]{1,0:T(1,128)}, u32[]{:S(2)}) copy-start(f32[1,128]{1,0:T(1,128)} %copy-done.83) | copy-start | bytes 1540 | tf_op jit(solution)/shard_map/while
  499.2 20.5 %copy-start.83 = (f32[1,128]{1,0:T(1,128)}, f32[1,128]{1,0:T(1,128)S(1)}, u32[]{:S(2)}) copy-start(f32[1,128]{1,0:T(1,128)S(1)} %get-tuple-element.602) | copy-start | bytes 1540 | tf_op jit(solution)/shard_map/while
  500.3 19.5 %copy-start.22 = (bf16[4,16384,8]{1,2,0:T(8,128)(2,1)S(1)}, bf16[4,16384,8]{1,2,0:T(8,128)(2,1)}, u32[]{:S(2)}) copy-start(bf16[4,16384,8]{1,2,0:T(8,128)(2,1)} %get-tuple-element.600) | copy-start | bytes 3145732 | tf_op jit(solution)/shard_map/while
  532.4 7.4 %copy-start.55 = (f32[128]{0:T(128)S(1)}, f32[128]{0:T(128)}, u32[]{:S(2)}) copy-start(f32[128]{0:T(128)} %get-tuple-element.581) | copy-start | bytes 1540 | tf_op jit(solution)/shard_map/while
  532.4 7.4 %copy-start.58 = (f32[128]{0:T(128)S(1)}, f32[128]{0:T(128)}, u32[]{:S(2)}) copy-start(f32[128]{0:T(128)} %get-tuple-element.580) | copy-start | bytes 1540 | tf_op jit(solution)/shard_map/while
  532.4 8.0 %copy-start.84 = (f32[1,128]{1,0:T(1,128)S(1)}, f32[1,128]{1,0:T(1,128)}, u32[]{:S(2)}) copy-start(f32[1,128]{1,0:T(1,128)} %copy-done.83) | copy-start | bytes 1540 | tf_op jit(solution)/shard_map/while
  540.6 6.9 copy-start.44
  549.8 21.5 %copy-start.67 = (f32[256]{0:T(256)S(1)}, f32[256]{0:T(256)}, u32[]{:S(2)}) copy-start(f32[256]{0:T(256)} %copy-done.66) | copy-start | bytes 3076
  549.8 21.5 %copy-start.72 = (f32[256]{0:T(256)S(1)}, f32[256]{0:T(256)}, u32[]{:S(2)}) copy-start(f32[256]{0:T(256)} %add_rsqrt_fusion) | copy-start | bytes 3076
  549.8 22.9 %copy-start.3 = (bf16[1024,768]{1,0:T(8,128)(2,1)S(1)}, bf16[1024,768]{1,0:T(8,128)(2,1)}, u32[]{:S(2)}) copy-start(bf16[1024,768]{1,0:T(8,128)(2,1)} %param.26) | copy-start | bytes 4718596
  549.8 22.9 %copy-start.42 = (f32[1024]{0:T(1024)S(1)}, f32[1024]{0:T(1024)}, u32[]{:S(2)}) copy-start(f32[1024]{0:T(1024)} %copy-done.40) | copy-start | bytes 12292
  549.8 22.9 %copy-start.49 = (f32[768]{0:T(1024)S(1)}, f32[768]{0:T(1024)}, u32[]{:S(2)}) copy-start(f32[768]{0:T(1024)} %param.31) | copy-start | bytes 9220
  578.4 117.4 %copy-start.1 = (bf16[3,768,192]{1,2,0:T(8,128)(2,1)S(1)}, bf16[3,768,192]{1,2,0:T(8,128)(2,1)}, u32[]{:S(2)}) copy-start(bf16[3,768,192]{1,2,0:T(8,128)(2,1)} %param.27) | copy-start | bytes 2654212
  (65 other events, 189.9 us)
Sparse Core Ops, SparseCore 0:
  206.7 44.8 all-reduce.9
  268.6 42.8 all-reduce.11
  353.2 68.3 all-reduce.17
  425.9 94.4 all-reduce.15
  572.7 121.4 all-reduce.13
where the time goes:
time: 708 us; the launch traced here: 702 us
  matrix products  279 us (39%)
  waiting for transfers between devices  139 us (20%)
  local copies, waits for them, and re-layouts  115 us (16%)
  other arithmetic  94.3 us (13%)
  blocking collectives  58.9 us (8%)
  between operations  15 us (2%)
    dot_general x4, matrix products, one_block(): return jnp.dot(hidden, kernel_w2, preferred_element_type=jnp.float32)  84.6 us
    dot_general x4, matrix products, one_block(): inner = jnp.dot(basis_b, kernel_w1, preferred_element_type=jnp.float32)  77.8 us
    psum x1, waiting for transfers between devices, body(): lax.psum((grad_kw1, grad_cen, grad_wid, grad_g1, grad_b1, grad_g2, grad_b...  62.5 us
    dynamic_update_slice x8, local copies, waits for them, and re-layouts, kernel_geo(): result = lax.map(one_block, dist_rows.reshape(total // block, block))  44.1 us
    psum x1, blocking collectives, body(): lax.psum((grad_kw1, grad_cen, grad_wid, grad_g1, grad_b1, grad_g2, grad_b...  40.9 us
    psum x1, waiting for transfers between devices, body(): lax.psum(attn_part.astype(jnp.bfloat16), 'tensor').astype(jnp.float32)  39.8 us
    psum x1, waiting for transfers between devices, body(): lax.psum(two_part.astype(jnp.bfloat16), 'tensor').astype(jnp.float32)  36.9 us
    reduce_sum x4, other arithmetic, kernels(): offset = (place - centers) / widths  29.6 us
  transfers between devices with their start and end apart: 5, of which 3 were waited for; matrix products, arithmetic and copies ran while one was open for 32% of the time, Pallas kernels for 0%

commit v1 on v0

--- a/solution.py
+++ b/solution.py
@@ -297,7 +297,7 @@
         lax.psum(grad_out.astype(jnp.bfloat16), "dp").astype(jnp.float32),
         lax.psum(grad_ff1.astype(jnp.bfloat16), "dp").astype(jnp.float32),
         lax.psum(grad_ff2.astype(jnp.bfloat16), "dp").astype(jnp.float32),
-        lax.psum(grad_spd.astype(jnp.bfloat16), "dp").astype(jnp.float32),
+        jnp.sum(lax.all_gather(grad_spd.astype(jnp.bfloat16), "dp"), axis=0).astype(jnp.float32),
         lax.psum(grad_edge.astype(jnp.bfloat16), "dp").astype(jnp.float32),
         lax.psum(grad_kw2.astype(jnp.bfloat16), "dp").astype(jnp.float32),
     )

time: 708 us -> 732 us (1.034)
  blocking collectives: 58.9 us -> 83.3 us
    all_gather x0 -> x1, blocking collectives: none -> 21.6 us  [body(): lax.all_gather(grad_spd.astype(jnp.bfloat16), 'dp')]
  transfers between devices with their start and end apart: 5 -> 5, of which waited for: 3 -> 3; matrix products, arithmetic and copies ran while one was open for 32% -> 31% of each run, Pallas kernels for 0% -> 0%
where the time goes in v1:
time: 732 us; the launch traced here: 727 us
  matrix products  279 us (38%)
  waiting for transfers between devices  139 us (19%)
  local copies, waits for them, and re-layouts  115 us (16%)
  other arithmetic  94.5 us (13%)
  blocking collectives  83.3 us (11%)
  between operations  15 us (2%)
    dot_general x4, matrix products, one_block(): return jnp.dot(hidden, kernel_w2, preferred_element_type=jnp.float32)  84.6 us
    dot_general x4, matrix products, one_block(): inner = jnp.dot(basis_b, kernel_w1, preferred_element_type=jnp.float32)  77.8 us
    psum x1, waiting for transfers between devices, body(): lax.psum((grad_kw1, grad_cen, grad_wid, grad_g1, grad_b1, grad_g2, grad_b...  62.6 us
    psum x1, blocking collectives, body(): lax.psum((grad_kw1, grad_cen, grad_wid, grad_g1, grad_b1, grad_g2, grad_b...  44.7 us
    dynamic_update_slice x8, local copies, waits for them, and re-layouts, kernel_geo(): result = lax.map(one_block, dist_rows.reshape(total // block, block))  44.4 us
    psum x1, waiting for transfers between devices, body(): lax.psum(attn_part.astype(jnp.bfloat16), 'tensor').astype(jnp.float32)  39.7 us
    psum x1, waiting for transfers between devices, body(): lax.psum(two_part.astype(jnp.bfloat16), 'tensor').astype(jnp.float32)  36.9 us
    reduce_sum x4, other arithmetic, kernels(): offset = (place - centers) / widths  29.6 us
  transfers between devices with their start and end apart: 5, of which 3 were waited for; matrix products, arithmetic and copies ran while one was open for 31% of the time, Pallas kernels for 0%

profile of v1, /device:TPU:1, one launch (start us, length us, event | category | flops | bytes accessed | tf_op | source)
XLA Modules:
  0.0 727.0 jit_solution(6240090821915042095)
XLA Ops:
  17.9 129.5 %while.6 = (s32[]{:T(128)}, f32[4,16384,8]{1,0,2:T(4,128)}, s32[4,16384]{1,0:T(4,128)S(1)}, f32[128]{0:T(128)S(1)}, f32[128]{0:T(128)S(1)}, /*index=5*/bf16[128,...) while((s32[]{:T(128)}, f32[4,16384,8]{1,0,2:T(4,128)}, s32[4,16384]{1,0:T(4,128)S(1)}, ...), condition=%wide.region_3.4_spmd, body=%wide.region_2.3_spmd.sunk | while | flops 719355904 | bytes 2853997 | solution.py:41
  18.2 21.2 %convolution_bitcast_fusion.2 = f32[1,16384,8]{1,2,0:T(8,128)S(1)} fusion(bf16[128,8]{0,1:T(8,128)(2,1)S(1)} %get-tuple-element.571, bf16[128,128]{1,0:T(8,128)(2,1)S(1)} %get-tuple-element.570, f32[128]{0:T(128)S(1)} %get-tuple-element.569, f32[128]{0:T(128)S(1)} %get-tuple-element.568, f32[16384]{0:T(1024)S(1)} %bitcast.184), kind=kOutput, calls=%fused_computation.clone.1 | convolution fusion | flops 719323136 | bytes 625664 | tf_op jit(solution)/shard_map/while/body/eval_jaxpr/dot_general | solution.py:39
  39.9 10.5 %dynamic_update_slice.20 = f32[4,16384,8]{1,0,2:T(4,128)} dynamic-update-slice(f32[4,16384,8]{1,0,2:T(4,128)} %get-tuple-element.557, f32[1,16384,8]{1,0,2:T(1,128)S(1)} %copy.156, s32[]{:T(128)S(6)} %copy.160, s32[]{:T(128)} %constant.312.clone.1..sunk, s32[]{:T(128)} %constant.312.clone.1..sunk) | dynamic-update-slice | bytes 1048580 | tf_op jit(solution)/shard_map/while/body/jit(dynamic_update_index_in_dim)/dynamic_update_slice | solution.py:41
  50.5 21.2 %convolution_bitcast_fusion.2 = f32[1,16384,8]{1,2,0:T(8,128)S(1)} fusion(bf16[128,8]{0,1:T(8,128)(2,1)S(1)} %get-tuple-element.571, bf16[128,128]{1,0:T(8,128)(2,1)S(1)} %get-tuple-element.570, f32[128]{0:T(128)S(1)} %get-tuple-element.569, f32[128]{0:T(128)S(1)} %get-tuple-element.568, f32[16384]{0:T(1024)S(1)} %bitcast.184), kind=kOutput, calls=%fused_computation.clone.1 | convolution fusion | flops 719323136 | bytes 625664 | tf_op jit(solution)/shard_map/while/body/eval_jaxpr/dot_general | solution.py:39
  72.2 10.5 %dynamic_update_slice.20 = f32[4,16384,8]{1,0,2:T(4,128)} dynamic-update-slice(f32[4,16384,8]{1,0,2:T(4,128)} %get-tuple-element.557, f32[1,16384,8]{1,0,2:T(1,128)S(1)} %copy.156, s32[]{:T(128)S(6)} %copy.160, s32[]{:T(128)} %constant.312.clone.1..sunk, s32[]{:T(128)} %constant.312.clone.1..sunk) | dynamic-update-slice | bytes 1048580 | tf_op jit(solution)/shard_map/while/body/jit(dynamic_update_index_in_dim)/dynamic_update_slice | solution.py:41
  82.9 21.2 %convolution_bitcast_fusion.2 = f32[1,16384,8]{1,2,0:T(8,128)S(1)} fusion(bf16[128,8]{0,1:T(8,128)(2,1)S(1)} %get-tuple-element.571, bf16[128,128]{1,0:T(8,128)(2,1)S(1)} %get-tuple-element.570, f32[128]{0:T(128)S(1)} %get-tuple-element.569, f32[128]{0:T(128)S(1)} %get-tuple-element.568, f32[16384]{0:T(1024)S(1)} %bitcast.184), kind=kOutput, calls=%fused_computation.clone.1 | convolution fusion | flops 719323136 | bytes 625664 | tf_op jit(solution)/shard_map/while/body/eval_jaxpr/dot_general | solution.py:39
  104.6 10.5 %dynamic_update_slice.20 = f32[4,16384,8]{1,0,2:T(4,128)} dynamic-update-slice(f32[4,16384,8]{1,0,2:T(4,128)} %get-tuple-element.557, f32[1,16384,8]{1,0,2:T(1,128)S(1)} %copy.156, s32[]{:T(128)S(6)} %copy.160, s32[]{:T(128)} %constant.312.clone.1..sunk, s32[]{:T(128)} %constant.312.clone.1..sunk) | dynamic-update-slice | bytes 1048580 | tf_op jit(solution)/shard_map/while/body/jit(dynamic_update_index_in_dim)/dynamic_update_slice | solution.py:41
  115.2 21.2 %convolution_bitcast_fusion.2 = f32[1,16384,8]{1,2,0:T(8,128)S(1)} fusion(bf16[128,8]{0,1:T(8,128)(2,1)S(1)} %get-tuple-element.571, bf16[128,128]{1,0:T(8,128)(2,1)S(1)} %get-tuple-element.570, f32[128]{0:T(128)S(1)} %get-tuple-element.569, f32[128]{0:T(128)S(1)} %get-tuple-element.568, f32[16384]{0:T(1024)S(1)} %bitcast.184), kind=kOutput, calls=%fused_computation.clone.1 | convolution fusion | flops 719323136 | bytes 625664 | tf_op jit(solution)/shard_map/while/body/eval_jaxpr/dot_general | solution.py:39
  136.9 10.5 %dynamic_update_slice.20 = f32[4,16384,8]{1,0,2:T(4,128)} dynamic-update-slice(f32[4,16384,8]{1,0,2:T(4,128)} %get-tuple-element.557, f32[1,16384,8]{1,0,2:T(1,128)S(1)} %copy.156, s32[]{:T(128)S(6)} %copy.160, s32[]{:T(128)} %constant.312.clone.1..sunk, s32[]{:T(128)} %constant.312.clone.1..sunk) | dynamic-update-slice | bytes 1048580 | tf_op jit(solution)/shard_map/while/body/jit(dynamic_update_index_in_dim)/dynamic_update_slice | solution.py:41
  148.1 5.0 squeeze.56
  153.1 5.5 copy.83
  163.5 7.7 %fusion.83 = f32[16,64,64,8]{2,3,1,0:T(8,128)} fusion(s32[16,64,64]{2,1,0:T(8,128)} %param.43, f32[32,8]{0,1:T(8,128)S(1)} %copy-done.68), kind=kOutput, calls=%fused_computation.114 | convolution fusion | flops 203423744 | bytes 2360320 | tf_op jit(solution)/shard_map/while/body/eval_jaxpr/dot_general | solution.py:87
  171.3 5.4 copy.80
  176.7 7.5 %fusion.82 = f32[16,64,64,8]{2,3,1,0:T(8,128)} fusion(s32[16,64,64]{2,1,0:T(8,128)} %param.44, f32[32,8]{0,1:T(8,128)S(1)} %copy-done.69), kind=kOutput, calls=%fused_computation.112 | convolution fusion | flops 203423744 | bytes 2360320 | tf_op jit(solution)/shard_map/while/body/eval_jaxpr/dot_general | solution.py:87
  184.2 5.4 copy.81
  189.6 8.2 %fusion.154 = (f32[16,8,64]{2,1,0:T(8,128)S(1)}, f32[16,8,64,64]{2,3,1,0:T(8,128)S(1)}, f32[16,64,64,8]{1,2,3,0:T(8,128)}, f32[16,8,64,64]{2,3,1,0:T(8,128)}) fusion(pred[16,64]{1,0:T(8,128)(4,1)S(1)} %copy-done.61, f32[16,64,64,8]{1,2,3,0:T(8,128)} %copy.83, f32[16]{0:T(128)S(1)} %copy-done.75, f32[16,64,64,8]{1,2,3,0:T(8,128)} %copy.80, ...), kind=kOutput, calls=%fused_computation.249 | convolution fusion | flops 28827648 | bytes 13403264 | tf_op jit(solution)/shard_map/while/body/eval_jaxpr/bihe,bjhe->bhij/dot_general | solution.py:97
  212.1 39.7 %all-reduce.10.cloned.1.call-done = bf16[1024,768]{1,0:T(8,128)(2,1)} async-done(((bf16[1024,768]{1,0:T(8,128)(2,1)}), bf16[1024,768]{1,0:T(8,128)(2,1)}) %all-reduce.10.cloned.1.call-update) | async-done | bytes 1572880 | tf_op jit(solution)/shard_map/psum | solution.py:230
  251.8 3.6 convert_add_fusion
  274.9 36.9 %all-reduce.12.cloned.1.call-done = bf16[1024,768]{1,0:T(8,128)(2,1)} async-done(((bf16[1024,768]{1,0:T(8,128)(2,1)}), bf16[1024,768]{1,0:T(8,128)(2,1)}) %all-reduce.12.cloned.1.call-update) | async-done | bytes 1572880 | tf_op jit(solution)/shard_map/psum | solution.py:244
  323.9 3.8 fusion.116
  353.4 6.6 broadcast_multiply_fusion.1
  361.6 4.0 copy.100
  375.9 164.8 %while.7 = (s32[]{:T(128)}, f32[128,128]{1,0:T(8,128)S(1)}, f32[128,8]{0,1:T(8,128)S(1)}, f32[128]{0:T(128)}, f32[128]{0:T(128)}, /*index=5*/s32[4,16384]{1,0:T(...) while((s32[]{:T(128)}, f32[128,128]{1,0:T(8,128)S(1)}, ...), condition=%wide.region_40.41_spmd.clone, body=%wide.region_36.40_spmd.clone.sunk | while | flops 1914768128 | bytes 101811056 | solution.py:72
  377.1 19.5 %fusion.219 = (f32[16384,128]{1,0:T(8,128)S(1)}, f32[16384,128]{1,0:T(8,128)S(1)}) fusion(bf16[128,128]{1,0:T(8,128)(2,1)S(1)} %get-tuple-element.610, f32[128]{0:T(128)S(1)} %get-tuple-element.609, f32[128]{0:T(128)S(1)} %get-tuple-element.608, f32[16384]{0:T(1024)S(1)} %bitcast.177), kind=kOutput, calls=%fused_computation.69.clone.1 | convolution fusion | flops 679477248 | bytes 16876544 | tf_op jit(solution)/shard_map/while/body/eval_jaxpr/dot_general | solution.py:55
  397.4 4.3 add_convert_fusion.9
  401.8 3.8 fusion.220
  405.5 3.6 fusion.222
  409.2 7.4 %fusion.223 = (f32[128]{0:T(128)S(1)}, f32[128]{0:T(128)S(1)}, f32[128]{0:T(128)S(1)}) fusion(f32[16384,128]{1,0:T(8,128)S(1)} %get-tuple-element.540, f32[128]{0:T(128)S(1)} %divide_bitcast_fusion.2, f32[128]{0:T(128)S(1)} %get-tuple-element.608, f32[16384]{0:T(1024)S(1)} %bitcast.180, f32[128]{0:T(128)S(1)} %get-tuple-element.609, ...), kind=kLoop, calls=%fused_computation.66.clone.1 | loop fusion | flops 25165440 | bytes 16845824 | tf_op jit(solution)/shard_map/while/body/eval_jaxpr/transpose(jvp())/reduce_sum | solution.py:26
  418.2 19.5 %fusion.219 = (f32[16384,128]{1,0:T(8,128)S(1)}, f32[16384,128]{1,0:T(8,128)S(1)}) fusion(bf16[128,128]{1,0:T(8,128)(2,1)S(1)} %get-tuple-element.610, f32[128]{0:T(128)S(1)} %get-tuple-element.609, f32[128]{0:T(128)S(1)} %get-tuple-element.608, f32[16384]{0:T(1024)S(1)} %bitcast.177), kind=kOutput, calls=%fused_computation.69.clone.1 | convolution fusion | flops 679477248 | bytes 16876544 | tf_op jit(solution)/shard_map/while/body/eval_jaxpr/dot_general | solution.py:55
  438.5 4.3 add_convert_fusion.9
  442.9 3.8 fusion.220
  446.6 3.6 fusion.222
  450.3 7.4 %fusion.223 = (f32[128]{0:T(128)S(1)}, f32[128]{0:T(128)S(1)}, f32[128]{0:T(128)S(1)}) fusion(f32[16384,128]{1,0:T(8,128)S(1)} %get-tuple-element.540, f32[128]{0:T(128)S(1)} %divide_bitcast_fusion.2, f32[128]{0:T(128)S(1)} %get-tuple-element.608, f32[16384]{0:T(1024)S(1)} %bitcast.180, f32[128]{0:T(128)S(1)} %get-tuple-element.609, ...), kind=kLoop, calls=%fused_computation.66.clone.1 | loop fusion | flops 25165440 | bytes 16845824 | tf_op jit(solution)/shard_map/while/body/eval_jaxpr/transpose(jvp())/reduce_sum | solution.py:26
  459.3 19.5 %fusion.219 = (f32[16384,128]{1,0:T(8,128)S(1)}, f32[16384,128]{1,0:T(8,128)S(1)}) fusion(bf16[128,128]{1,0:T(8,128)(2,1)S(1)} %get-tuple-element.610, f32[128]{0:T(128)S(1)} %get-tuple-element.609, f32[128]{0:T(128)S(1)} %get-tuple-element.608, f32[16384]{0:T(1024)S(1)} %bitcast.177), kind=kOutput, calls=%fused_computation.69.clone.1 | convolution fusion | flops 679477248 | bytes 16876544 | tf_op jit(solution)/shard_map/while/body/eval_jaxpr/dot_general | solution.py:55
  479.7 4.3 add_convert_fusion.9
  484.0 3.8 fusion.220
  487.8 3.6 fusion.222
  491.4 7.4 %fusion.223 = (f32[128]{0:T(128)S(1)}, f32[128]{0:T(128)S(1)}, f32[128]{0:T(128)S(1)}) fusion(f32[16384,128]{1,0:T(8,128)S(1)} %get-tuple-element.540, f32[128]{0:T(128)S(1)} %divide_bitcast_fusion.2, f32[128]{0:T(128)S(1)} %get-tuple-element.608, f32[16384]{0:T(1024)S(1)} %bitcast.180, f32[128]{0:T(128)S(1)} %get-tuple-element.609, ...), kind=kLoop, calls=%fused_computation.66.clone.1 | loop fusion | flops 25165440 | bytes 16845824 | tf_op jit(solution)/shard_map/while/body/eval_jaxpr/transpose(jvp())/reduce_sum | solution.py:26
  500.5 19.5 %fusion.219 = (f32[16384,128]{1,0:T(8,128)S(1)}, f32[16384,128]{1,0:T(8,128)S(1)}) fusion(bf16[128,128]{1,0:T(8,128)(2,1)S(1)} %get-tuple-element.610, f32[128]{0:T(128)S(1)} %get-tuple-element.609, f32[128]{0:T(128)S(1)} %get-tuple-element.608, f32[16384]{0:T(1024)S(1)} %bitcast.177), kind=kOutput, calls=%fused_computation.69.clone.1 | convolution fusion | flops 679477248 | bytes 16876544 | tf_op jit(solution)/shard_map/while/body/eval_jaxpr/dot_general | solution.py:55
  520.8 4.3 add_convert_fusion.9
  525.1 3.8 fusion.220
  528.9 3.6 fusion.222
  532.6 7.4 %fusion.223 = (f32[128]{0:T(128)S(1)}, f32[128]{0:T(128)S(1)}, f32[128]{0:T(128)S(1)}) fusion(f32[16384,128]{1,0:T(8,128)S(1)} %get-tuple-element.540, f32[128]{0:T(128)S(1)} %divide_bitcast_fusion.2, f32[128]{0:T(128)S(1)} %get-tuple-element.608, f32[16384]{0:T(1024)S(1)} %bitcast.180, f32[128]{0:T(128)S(1)} %get-tuple-element.609, ...), kind=kLoop, calls=%fused_computation.66.clone.1 | loop fusion | flops 25165440 | bytes 16845824 | tf_op jit(solution)/shard_map/while/body/eval_jaxpr/transpose(jvp())/reduce_sum | solution.py:26
  543.6 4.0 fusion.124
  547.6 21.6 %all-gather.1 = bf16[8,32,8]{1,2,0:T(8,128)(2,1)S(1)} all-gather(bf16[1,32,8]{1,2,0:T(8,128)(2,1)S(1)} %fusion.124), channel_id=2, replica_groups=mesh['dp'=8,'tensor'=4] {'dp'}, dimensions={0}, use_global_device_ids=true | all-gather | bytes 4608 | tf_op jit(solution)/shard_map/all_gather | solution.py:300
  572.1 17.0 %all-reduce.1 = (bf16[32,8]{0,1:T(8,128)(2,1)S(1)}, bf16[128,8]{0,1:T(8,128)(2,1)S(1)}) all-reduce(bf16[32,8]{0,1:T(8,128)(2,1)S(1)} %fusion.123, bf16[128,8]{0,1:T(8,128)(2,1)S(1)} %convert_element_type.294), channel_id=1, replica_groups=mesh['dp'=8,'tensor'=4] {'dp'}, use_global_device_ids=true, to_apply=%region_35.36 | all-reduce | flops 1280 | bytes 5120 | tf_op jit(solution)/shard_map/psum | solution.py:301
  603.6 44.7 %all-reduce = (f32[768]{0:T(1024)}, f32[768]{0:T(1024)}, f32[768]{0:T(1024)}, f32[768]{0:T(1024)}, f32[128]{0:T(128)}, /*index=5*/f32[128]{0:T(128)}) all-reduce(f32[768]{0:T(1024)S(1)} %get-tuple-element.332, f32[768]{0:T(1024)S(1)} %get-tuple-element.331, ...), channel_id=1, replica_groups=mesh['dp'=8,'tensor'=4] {'dp','tensor'}, use_global_device_ids=true, to_apply=%region_25.26 | all-reduce | flops 3328 | bytes 26624 | tf_op jit(solution)/shard_map/psum | solution.py:304
  656.3 62.6 %all-reduce.14.cloned.1.call-done = f32[128,128]{1,0:T(8,128)} async-done(((f32[128,128]{1,0:T(8,128)}), f32[128,128]{1,0:T(8,128)}) %all-reduce.14.cloned.1.call-update) | async-done | bytes 65552 | tf_op jit(solution)/shard_map/psum | solution.py:304
  (345 shorter events, 140.9 us)
Async XLA Ops:
  7.2 244.6 %all-reduce.10.cloned.1.call-start = ((), (), s32[]{:S(2)}) async-start(), calls=%async_computation | async-start | bytes 3145728 | tf_op jit(solution)/shard_map/psum | solution.py:230
  160.0 39.1 %copy-start.26 = (bf16[16,64,8,24]{1,0,3,2:T(8,128)(2,1)}, bf16[16,64,8,24]{1,0,3,2:T(8,128)(2,1)S(1)}, u32[]{:S(2)}) copy-start(bf16[16,64,8,24]{1,0,3,2:T(8,128)(2,1)S(1)} %convert_element_type.241) | copy-start | bytes 1179652
  163.5 26.0 %copy-start.18 = (bf16[16,64,8,24]{1,0,3,2:T(8,128)(2,1)}, bf16[16,64,8,24]{1,0,3,2:T(8,128)(2,1)S(1)}, u32[]{:S(2)}) copy-start(bf16[16,64,8,24]{1,0,3,2:T(8,128)(2,1)S(1)} %convert_element_type.244) | copy-start | bytes 1179652
  206.8 105.0 %all-reduce.12.cloned.1.call-start = ((), (), s32[]{:S(2)}) async-start(), calls=%async_computation.1 | async-start | bytes 3145728 | tf_op jit(solution)/shard_map/psum | solution.py:244
  210.1 46.1 %copy-start.64 = (f32[256]{0:T(256)}, f32[256]{0:T(256)S(1)}, u32[]{:S(2)}) copy-start(f32[256]{0:T(256)S(1)} %broadcast_multiply_fusion.5) | copy-start | bytes 3076
  212.1 44.2 %copy-start.45 = (f32[768]{0:T(1024)S(1)}, f32[768]{0:T(1024)}, u32[]{:S(2)}) copy-start(f32[768]{0:T(1024)} %param.33) | copy-start | bytes 9220
  212.1 44.2 %copy-start.70 = (f32[768]{0:T(1024)S(1)}, f32[768]{0:T(1024)}, u32[]{:S(2)}) copy-start(f32[768]{0:T(1024)} %param.34) | copy-start | bytes 9220
  265.1 9.8 %copy-start.66 = (f32[256]{0:T(256)}, f32[256]{0:T(256)S(1)}, u32[]{:S(2)}) copy-start(f32[256]{0:T(256)S(1)} %broadcast_multiply_fusion.4) | copy-start | bytes 3076
  268.7 324.7 %all-reduce.18.cloned.1.call-start = ((), (), s32[]{:S(2)}) async-start(), calls=%async_computation.4 | async-start | bytes 6291456 | tf_op jit(solution)/shard_map/psum | solution.py:236
  333.5 10.3 %copy-start.28 = (bf16[16,64,8,24]{1,3,2,0:T(8,128)(2,1)S(1)}, bf16[16,64,8,24]{1,3,2,0:T(8,128)(2,1)}, u32[]{:S(2)}) copy-start(bf16[16,64,8,24]{1,3,2,0:T(8,128)(2,1)} %fusion.115) | copy-start | bytes 1179652
  338.9 11.7 %copy-start.86 = (f32[3]{0:T(128)S(1)}, f32[3]{0:T(128)}, u32[]{:S(2)}) copy-start(f32[3]{0:T(128)} %constant.350.clone) | copy-start | bytes 40
  353.3 295.0 %all-reduce.16.cloned.1.call-start = ((), (), s32[]{:S(2)}) async-start(), calls=%async_computation.3 | async-start | bytes 3538944 | tf_op jit(solution)/shard_map/psum | solution.py:296
  361.6 9.2 %copy-start.23 = (bf16[1024,192]{0,1:T(8,128)(2,1)S(1)}, bf16[1024,192]{0,1:T(8,128)(2,1)}, u32[]{:S(2)}) copy-start(bf16[1024,192]{0,1:T(8,128)(2,1)} %reshape.250) | copy-start | bytes 1179652
  365.6 7.8 %copy-start.41 = (f32[1024]{0:T(1024)S(1)}, f32[1024]{0:T(1024)}, u32[]{:S(2)}) copy-start(f32[1024]{0:T(1024)} %copy-done.40) | copy-start | bytes 12292
  365.6 7.8 %copy-start.48 = (f32[768]{0:T(1024)S(1)}, f32[768]{0:T(1024)}, u32[]{:S(2)}) copy-start(f32[768]{0:T(1024)} %param.31) | copy-start | bytes 9220
  365.6 7.8 %copy-start.51 = (f32[1024]{0:T(1024)S(1)}, f32[1024]{0:T(1024)}, u32[]{:S(2)}) copy-start(f32[1024]{0:T(1024)} %copy-done.50) | copy-start | bytes 12292
  365.6 7.8 %copy-start.81 = (f32[768]{0:T(1024)S(1)}, f32[768]{0:T(1024)}, u32[]{:S(2)}) copy-start(f32[768]{0:T(1024)} %param.32) | copy-start | bytes 9220
  375.8 343.1 %all-reduce.14.cloned.1.call-start = ((), (), s32[]{:S(2)}) async-start(), calls=%async_computation.2 | async-start | bytes 131072 | tf_op jit(solution)/shard_map/psum | solution.py:304
  375.8 164.9 %copy-start.17 = (bf16[16,64,64,8]{1,2,3,0:T(8,128)(2,1)S(1)}, bf16[16,64,64,8]{1,2,3,0:T(8,128)(2,1)}, u32[]{:S(2)}) copy-start(bf16[16,64,64,8]{1,2,3,0:T(8,128)(2,1)} %get-tuple-element.385) | copy-start | bytes 3145732
  375.9 20.7 %copy-start.84 = (f32[1,128]{1,0:T(1,128)}, f32[1,128]{1,0:T(1,128)S(1)}, u32[]{:S(2)}) copy-start(f32[1,128]{1,0:T(1,128)S(1)} %get-tuple-element.613) | copy-start | bytes 1540 | tf_op jit(solution)/shard_map/while
  377.1 19.5 %copy-start.22 = (bf16[4,16384,8]{1,2,0:T(8,128)(2,1)S(1)}, bf16[4,16384,8]{1,2,0:T(8,128)(2,1)}, u32[]{:S(2)}) copy-start(bf16[4,16384,8]{1,2,0:T(8,128)(2,1)} %get-tuple-element.611) | copy-start | bytes 3145732 | tf_op jit(solution)/shard_map/while
  409.1 7.4 %copy-start.55 = (f32[128]{0:T(128)S(1)}, f32[128]{0:T(128)}, u32[]{:S(2)}) copy-start(f32[128]{0:T(128)} %get-tuple-element.592) | copy-start | bytes 1540 | tf_op jit(solution)/shard_map/while
  409.2 7.4 %copy-start.58 = (f32[128]{0:T(128)S(1)}, f32[128]{0:T(128)}, u32[]{:S(2)}) copy-start(f32[128]{0:T(128)} %get-tuple-element.591) | copy-start | bytes 1540 | tf_op jit(solution)/shard_map/while
  409.2 8.0 %copy-start.85 = (f32[1,128]{1,0:T(1,128)S(1)}, f32[1,128]{1,0:T(1,128)}, u32[]{:S(2)}) copy-start(f32[1,128]{1,0:T(1,128)} %copy-done.84) | copy-start | bytes 1540 | tf_op jit(solution)/shard_map/while
  417.2 20.5 %copy-start.84 = (f32[1,128]{1,0:T(1,128)}, f32[1,128]{1,0:T(1,128)S(1)}, u32[]{:S(2)}) copy-start(f32[1,128]{1,0:T(1,128)S(1)} %get-tuple-element.613) | copy-start | bytes 1540 | tf_op jit(solution)/shard_map/while
  418.2 19.5 %copy-start.22 = (bf16[4,16384,8]{1,2,0:T(8,128)(2,1)S(1)}, bf16[4,16384,8]{1,2,0:T(8,128)(2,1)}, u32[]{:S(2)}) copy-start(bf16[4,16384,8]{1,2,0:T(8,128)(2,1)} %get-tuple-element.611) | copy-start | bytes 3145732 | tf_op jit(solution)/shard_map/while
  450.3 7.4 %copy-start.55 = (f32[128]{0:T(128)S(1)}, f32[128]{0:T(128)}, u32[]{:S(2)}) copy-start(f32[128]{0:T(128)} %get-tuple-element.592) | copy-start | bytes 1540 | tf_op jit(solution)/shard_map/while
  450.3 7.4 %copy-start.58 = (f32[128]{0:T(128)S(1)}, f32[128]{0:T(128)}, u32[]{:S(2)}) copy-start(f32[128]{0:T(128)} %get-tuple-element.591) | copy-start | bytes 1540 | tf_op jit(solution)/shard_map/while
  450.3 8.0 %copy-start.85 = (f32[1,128]{1,0:T(1,128)S(1)}, f32[1,128]{1,0:T(1,128)}, u32[]{:S(2)}) copy-start(f32[1,128]{1,0:T(1,128)} %copy-done.84) | copy-start | bytes 1540 | tf_op jit(solution)/shard_map/while
  458.3 20.5 %copy-start.84 = (f32[1,128]{1,0:T(1,128)}, f32[1,128]{1,0:T(1,128)S(1)}, u32[]{:S(2)}) copy-start(f32[1,128]{1,0:T(1,128)S(1)} %get-tuple-element.613) | copy-start | bytes 1540 | tf_op jit(solution)/shard_map/while
  459.3 19.5 %copy-start.22 = (bf16[4,16384,8]{1,2,0:T(8,128)(2,1)S(1)}, bf16[4,16384,8]{1,2,0:T(8,128)(2,1)}, u32[]{:S(2)}) copy-start(bf16[4,16384,8]{1,2,0:T(8,128)(2,1)} %get-tuple-element.611) | copy-start | bytes 3145732 | tf_op jit(solution)/shard_map/while
  491.4 7.4 %copy-start.55 = (f32[128]{0:T(128)S(1)}, f32[128]{0:T(128)}, u32[]{:S(2)}) copy-start(f32[128]{0:T(128)} %get-tuple-element.592) | copy-start | bytes 1540 | tf_op jit(solution)/shard_map/while
  491.4 7.4 %copy-start.58 = (f32[128]{0:T(128)S(1)}, f32[128]{0:T(128)}, u32[]{:S(2)}) copy-start(f32[128]{0:T(128)} %get-tuple-element.591) | copy-start | bytes 1540 | tf_op jit(solution)/shard_map/while
  491.4 8.0 %copy-start.85 = (f32[1,128]{1,0:T(1,128)S(1)}, f32[1,128]{1,0:T(1,128)}, u32[]{:S(2)}) copy-start(f32[1,128]{1,0:T(1,128)} %copy-done.84) | copy-start | bytes 1540 | tf_op jit(solution)/shard_map/while
  499.4 20.5 %copy-start.84 = (f32[1,128]{1,0:T(1,128)}, f32[1,128]{1,0:T(1,128)S(1)}, u32[]{:S(2)}) copy-start(f32[1,128]{1,0:T(1,128)S(1)} %get-tuple-element.613) | copy-start | bytes 1540 | tf_op jit(solution)/shard_map/while
  500.4 19.5 %copy-start.22 = (bf16[4,16384,8]{1,2,0:T(8,128)(2,1)S(1)}, bf16[4,16384,8]{1,2,0:T(8,128)(2,1)}, u32[]{:S(2)}) copy-start(bf16[4,16384,8]{1,2,0:T(8,128)(2,1)} %get-tuple-element.611) | copy-start | bytes 3145732 | tf_op jit(solution)/shard_map/while
  532.5 7.4 %copy-start.55 = (f32[128]{0:T(128)S(1)}, f32[128]{0:T(128)}, u32[]{:S(2)}) copy-start(f32[128]{0:T(128)} %get-tuple-element.592) | copy-start | bytes 1540 | tf_op jit(solution)/shard_map/while
  532.5 7.4 %copy-start.58 = (f32[128]{0:T(128)S(1)}, f32[128]{0:T(128)}, u32[]{:S(2)}) copy-start(f32[128]{0:T(128)} %get-tuple-element.591) | copy-start | bytes 1540 | tf_op jit(solution)/shard_map/while
  532.5 8.0 %copy-start.85 = (f32[1,128]{1,0:T(1,128)S(1)}, f32[1,128]{1,0:T(1,128)}, u32[]{:S(2)}) copy-start(f32[1,128]{1,0:T(1,128)} %copy-done.84) | copy-start | bytes 1540 | tf_op jit(solution)/shard_map/while
  540.7 6.9 copy-start.44
  543.6 26.2 %copy-start.30 = (bf16[16,64,64,8]{2,3,1,0:T(8,128)(2,1)S(1)}, bf16[16,64,64,8]{2,3,1,0:T(8,128)(2,1)}, u32[]{:S(2)}) copy-start(bf16[16,64,64,8]{2,3,1,0:T(8,128)(2,1)} %copy.98) | copy-start | bytes 3145732
  543.6 26.2 %copy-start.32 = (s32[16,64,64]{2,1,0:T(8,128)S(1)}, s32[16,64,64]{2,1,0:T(8,128)}, u32[]{:S(2)}) copy-start(s32[16,64,64]{2,1,0:T(8,128)} %param.44) | copy-start | bytes 786436
  572.1 19.9 %copy-start.67 = (f32[256]{0:T(256)S(1)}, f32[256]{0:T(256)}, u32[]{:S(2)}) copy-start(f32[256]{0:T(256)} %copy-done.66) | copy-start | bytes 3076
  572.1 19.9 %copy-start.72 = (f32[256]{0:T(256)S(1)}, f32[256]{0:T(256)}, u32[]{:S(2)}) copy-start(f32[256]{0:T(256)} %add_rsqrt_fusion) | copy-start | bytes 3076
  572.1 21.3 %copy-start.3 = (bf16[1024,768]{1,0:T(8,128)(2,1)S(1)}, bf16[1024,768]{1,0:T(8,128)(2,1)}, u32[]{:S(2)}) copy-start(bf16[1024,768]{1,0:T(8,128)(2,1)} %param.26) | copy-start | bytes 4718596
  572.1 21.3 %copy-start.42 = (f32[1024]{0:T(1024)S(1)}, f32[1024]{0:T(1024)}, u32[]{:S(2)}) copy-start(f32[1024]{0:T(1024)} %copy-done.40) | copy-start | bytes 12292
  572.1 21.3 %copy-start.49 = (f32[768]{0:T(1024)S(1)}, f32[768]{0:T(1024)}, u32[]{:S(2)}) copy-start(f32[768]{0:T(1024)} %param.31) | copy-start | bytes 9220
  599.1 121.2 %copy-start.1 = (bf16[3,768,192]{1,2,0:T(8,128)(2,1)S(1)}, bf16[3,768,192]{1,2,0:T(8,128)(2,1)}, u32[]{:S(2)}) copy-start(bf16[3,768,192]{1,2,0:T(8,128)(2,1)} %param.27) | copy-start | bytes 2654212
  (65 other events, 190.7 us)
Sparse Core Ops, SparseCore 0:
  206.9 44.8 all-reduce.9
  268.9 42.8 all-reduce.11
  353.5 68.3 all-reduce.17
  426.2 94.4 all-reduce.15
  593.5 125.2 all-reduce.13
